TPU v7x, 32 devices: a whole 2x2x4 slice. The times are simulated.
32 devices in a mesh: group: 4 (over x, core), dev: 8 (over z, y).
Axes of the slice: x: 2, y: 2, z: 4, core: 2. Of those that a mesh axis runs over, the one named last changes fastest.
Arguments:
- features: bfloat16 [131072, 128], P(('group', 'dev')), may hold values from -6 to 6
- coords: bfloat16 [3, 131072], P(None, ('group', 'dev')), may hold values from 0 to 1
- near_pairs: int32 [2, 256], P(None, 'group'), may hold values from 0 to 127, as said below
- parent_two: int32 [512], P(('group', 'dev')), may hold values from 0 to 31, as said below
- parent_three: int32 [128], P('group'), may hold values from 0 to 7
- rates: float32 [4], replicated, may hold values from 6 to 40
- w_near: bfloat16 [128, 128], replicated, may hold values from -0.5 to 0.5
- restrict: bfloat16 [64, 256], replicated, may hold values from -0.375 to 0.375
- w_two: bfloat16 [128, 128], replicated, may hold values from -0.5 to 0.5
- w_three: bfloat16 [128, 128], replicated, may hold values from -0.5 to 0.5
- w_four: bfloat16 [128, 128], replicated, may hold values from -0.5 to 0.5
- coupling: bfloat16 [32, 32], replicated, may hold values from -1 to 1
- expand: bfloat16 [256, 64], replicated, may hold values from -0.75 to 0.75
- w_out: bfloat16 [128, 128], replicated, may hold values from -0.5 to 0.5
Outputs:
- mixed: bfloat16 [131072, 128], P(('group', 'dev'))
Inputs may be any that keep to these rules, and one draw needn't show every extreme that they name: `near_pairs`: for any two devices A and P of dev in one region, at most 2 near pairs of that region have their first block on A and their second on P, and in each region some such two devices have exactly 2. `parent_two`: every level-two node of a region is named by exactly four blocks of that region.
All inputs are finite; a program needn't handle non-finite values.
Results may differ from a plain program's by a relative error of at most 0.008.
Values may be sent and summed in bfloat16 or wider, within the bound.
A program may use at most 128 MiB of HBM per device.

v0:
```python
import jax
import jax.numpy as jnp
from jax import lax
from jax.sharding import PartitionSpec as P

CAP = 2
NODES3_GROUP = 8


def kernel_table(cloud_one, cloud_two, rates):
    first_pos = cloud_one.astype(jnp.float32)
    second_pos = cloud_two.astype(jnp.float32)
    delta_x = first_pos[:, 0, :, None] - second_pos[:, 0, None, :]
    delta_y = first_pos[:, 1, :, None] - second_pos[:, 1, None, :]
    delta_z = first_pos[:, 2, :, None] - second_pos[:, 2, None, :]
    distance = delta_x * delta_x + delta_y * delta_y + delta_z * delta_z
    return jnp.exp(-rates[None, :, None, None] * distance[:, None]).astype(jnp.bfloat16)


def apply_table(kernel, block_values, head_count, transposed):
    channels = block_values.shape[-1]
    head_of = jnp.arange(channels, dtype=jnp.int32) // (channels // head_count)
    head_mask = (head_of[None, :] == jnp.arange(head_count, dtype=jnp.int32)[:, None]).astype(
        jnp.bfloat16
    )
    masked = block_values[:, None, :, :] * head_mask[None, :, None, :]
    form = "nhqp,nhqc->npc" if transposed else "nhpq,nhqc->npc"
    return jnp.einsum(form, kernel, masked, preferred_element_type=jnp.float32)


def in_groups(array):
    return array.reshape((array.shape[0] // 8, 8) + array.shape[1:])


def per_device(
    features,
    coords,
    near_pairs,
    parent_two,
    parent_three,
    rates,
    w_near,
    restrict,
    w_two,
    w_three,
    w_four,
    coupling,
    expand,
    w_out,
):
    dev_count = lax.axis_size("dev")
    dev_index = lax.axis_index("dev")
    group_index = lax.axis_index("group")
    points_n, channels = features.shape
    blk_points = expand.shape[0]
    summary_rows = expand.shape[1]
    block_count = points_n // blk_points
    head_count = rates.shape[0]
    block_range = jnp.arange(block_count, dtype=jnp.int32)
    values = jnp.dot(features, w_near, preferred_element_type=jnp.float32).astype(jnp.bfloat16)
    vblocks = values.reshape(block_count, blk_points, channels)
    cblocks = coords.reshape(3, block_count, blk_points).transpose(1, 0, 2)

    def self_term(operands):
        cloud, block_values = operands
        return apply_table(kernel_table(cloud, cloud, rates), block_values, head_count, False)

    near_field = lax.map(
        self_term,
        (cblocks.reshape(-1, 4, 3, blk_points), vblocks.reshape(-1, 4, blk_points, channels)),
    )
    near_field = near_field.reshape(block_count, blk_points * channels)
    first_block = near_pairs[0]
    second_block = near_pairs[1]
    owner_first = first_block // block_count
    owner_second = second_block // block_count
    pair_key = owner_first * dev_count + owner_second
    position = jnp.arange(first_block.shape[0], dtype=jnp.int32)
    slot_rank = jnp.sum(
        (pair_key[:, None] == pair_key[None, :]) & (position[None, :] < position[:, None]), axis=1
    )
    slot_rows = dev_count * CAP
    row_range = jnp.arange(slot_rows, dtype=jnp.int32)
    peer_of_row = row_range // CAP
    slot_of_row = row_range % CAP
    same_slot = slot_rank[None, :] == slot_of_row[:, None]
    match_first = (
        (owner_first[None, :] == dev_index)
        & (owner_second[None, :] == peer_of_row[:, None])
        & same_slot
    )
    match_second = (
        (owner_first[None, :] == peer_of_row[:, None])
        & (owner_second[None, :] == dev_index)
        & same_slot
    )
    live_first = jnp.any(match_first, axis=1)
    live_second = jnp.any(match_second, axis=1)
    index_first = jnp.sum(jnp.where(match_first, first_block[None, :] % block_count, 0), axis=1)
    index_second = jnp.sum(jnp.where(match_second, second_block[None, :] % block_count, 0), axis=1)
    weight = live_second.astype(jnp.bfloat16)
    picked_values = (vblocks[index_second] * weight[:, None, None]).reshape(
        dev_count, CAP, blk_points, channels
    )
    picked_coords = (cblocks[index_second] * weight[:, None, None]).reshape(
        dev_count, CAP, 3, blk_points
    )
    mine_values = vblocks[index_first]
    mine_coords = cblocks[index_first]
    onehot_second = ((index_second[None, :] == block_range[:, None]) & live_second[None, :]).astype(
        jnp.bfloat16
    )

    def accumulate(running, side, index, live_rows):
        flat_side = side.reshape(side.shape[0], -1) * live_rows[:, None]
        return running.at[index].add(flat_side)

    got_values, got_coords = (
        lax.all_to_all(picked_values, "dev", split_axis=0, concat_axis=0, tiled=True),
        lax.all_to_all(picked_coords, "dev", split_axis=0, concat_axis=0, tiled=True),
    )
    got_values = got_values.reshape(slot_rows, blk_points, channels)
    got_coords = got_coords.reshape(slot_rows, 3, blk_points)

    def pair_step(running, operands):
        first_pos, second_pos, first_vals, second_vals, index, live_rows = operands
        kernel = kernel_table(first_pos, second_pos, rates)
        side_first = apply_table(kernel, second_vals, head_count, False)
        side_second = apply_table(kernel, first_vals, head_count, True) * live_rows[:, None, None]
        return (accumulate(running, side_first, index, live_rows), side_second.astype(jnp.bfloat16))

    near_field, side_second = lax.scan(
        pair_step,
        near_field,
        (
            in_groups(mine_coords),
            in_groups(got_coords),
            in_groups(mine_values),
            in_groups(got_values),
            in_groups(index_first),
            in_groups(live_first.astype(jnp.float32)),
        ),
    )
    returned = lax.all_to_all(
        side_second.reshape(dev_count, CAP, blk_points, channels),
        "dev",
        split_axis=0,
        concat_axis=0,
        tiled=True,
    )
    near_field = near_field + jnp.dot(
        onehot_second, returned.reshape(slot_rows, -1), preferred_element_type=jnp.float32
    )
    level_one = jnp.einsum(
        "sb,nbc->nsc",
        restrict,
        features.reshape(block_count, blk_points, channels),
        preferred_element_type=jnp.float32,
    )
    level_one = level_one.astype(jnp.bfloat16).reshape(block_count, summary_rows * channels)
    nodes_group = parent_three.shape[0]
    coarse_range = jnp.arange(NODES3_GROUP, dtype=jnp.int32)
    coarse_scale = NODES3_GROUP / nodes_group
    select_all = (parent_two[None, :] == jnp.arange(nodes_group, dtype=jnp.int32)[:, None]).astype(
        jnp.bfloat16
    )
    partial_two = jnp.dot(select_all, level_one, preferred_element_type=jnp.float32)
    flat = lax.psum(partial_two, "dev").astype(jnp.bfloat16).reshape(-1, channels)
    result = jax.nn.gelu(jnp.dot(flat, w_two, preferred_element_type=jnp.float32)).astype(
        jnp.bfloat16
    )
    level_two = result.reshape(-1, summary_rows * channels)
    select = (parent_three[None, :] == coarse_range[:, None]).astype(jnp.bfloat16)
    level_three = jnp.dot(select, level_two, preferred_element_type=jnp.float32)
    level_three = (level_three * coarse_scale).astype(jnp.bfloat16)
    three_all = lax.all_gather(level_three, "group", axis=0, tiled=True)
    coupling_rows = lax.dynamic_slice_in_dim(coupling, group_index * NODES3_GROUP, NODES3_GROUP, 0)
    mixed_three = jnp.dot(coupling_rows, three_all, preferred_element_type=jnp.float32).astype(
        jnp.bfloat16
    )
    down_three = jax.nn.gelu(
        jnp.dot(mixed_three.reshape(-1, channels), w_three, preferred_element_type=jnp.float32)
    )
    down_three = down_three.astype(jnp.bfloat16).reshape(NODES3_GROUP, summary_rows * channels)
    lift_table = (parent_three[:, None] == coarse_range[None, :]).astype(jnp.bfloat16)
    lifted = jnp.dot(
        level_two.reshape(-1, channels), w_four, preferred_element_type=jnp.float32
    ).reshape(-1, summary_rows * channels)
    down_two = jax.nn.gelu(
        lifted + jnp.dot(lift_table, down_three, preferred_element_type=jnp.float32)
    ).astype(jnp.bfloat16)
    select_parent = (
        parent_two[:, None] == jnp.arange(nodes_group, dtype=jnp.int32)[None, :]
    ).astype(jnp.bfloat16)
    parent_down = jnp.dot(select_parent, down_two, preferred_element_type=jnp.float32).astype(
        jnp.bfloat16
    )
    far_field = jnp.einsum(
        "bs,nsc->nbc",
        expand,
        parent_down.reshape(block_count, summary_rows, channels),
        preferred_element_type=jnp.float32,
    )
    far_field = far_field.astype(jnp.bfloat16).reshape(points_n, channels)
    total = near_field.reshape(points_n, channels) * blk_points ** (-0.5) + jnp.dot(
        far_field, w_out, preferred_element_type=jnp.float32
    )
    return total.astype(jnp.bfloat16)


def solution(mesh):
    placed = (
        P(("group", "dev"), None),
        P(None, ("group", "dev")),
        P(None, "group"),
        P(("group", "dev")),
        P("group"),
        P(),
        P(),
        P(),
        P(),
        P(),
        P(),
        P(),
        P(),
        P(),
    )
    return jax.shard_map(
        per_device, mesh=mesh, in_specs=placed, out_specs=P(("group", "dev"), None), check_vma=False
    )
```

profile of v0, /device:TPU:0, one launch (start us, length us, event | category | flops | bytes accessed | tf_op | source)
XLA Modules:
  0.0 172.9 jit_solution(7993352973277343777)
XLA Ops:
  4.3 7.3 %all-to-all-start = ((bf16[8,2,3,256]{3,1,2,0:T(2,128)(2,1)}), bf16[8,2,3,256]{3,1,2,0:T(2,128)(2,1)S(1)}, u32[]{:S(2)}, u32[]{:S(2)}) async-start(bf16[8,2,3,256]{3,1,2,0:T(2,128)(2,1)} %copy_multiply_fusion), calls=%async_computation | async-start | bytes 49152 | tf_op jit(solution)/shard_map/all_to_all | solution.py:120
  14.8 3.5 %all-to-all-done = bf16[8,2,3,256]{3,1,2,0:T(2,128)(2,1)S(1)} async-done(((bf16[8,2,3,256]{3,1,2,0:T(2,128)(2,1)}), bf16[8,2,3,256]{3,1,2,0:T(2,128)(2,1)S(1)}, u32[]{:S(2)}, u32[]{:S(2)}) %all-to-all-start) | async-done | bytes 24608 | tf_op jit(solution)/shard_map/all_to_all | solution.py:120
  18.3 4.2 %all-to-all-start.1 = ((bf16[8,2,256,128]{3,2,1,0:T(8,128)(2,1)}), bf16[8,2,256,128]{3,2,1,0:T(8,128)(2,1)}, u32[]{:S(2)}, u32[]{:S(2)}) async-start(bf16[8,2,256,128]{3,2,1,0:T(8,128)(2,1)} %broadcast_multiply_fusion), calls=%async_computation.1 | async-start | bytes 2097152 | tf_op jit(solution)/shard_map/all_to_all | solution.py:119
  22.5 8.8 %while.26 = (s32[]{:T(128)}, f32[4,4,256,128]{3,2,1,0:T(8,128)}, f32[1,4,1,1]{1,3,2,0:T(1,128)S(1)}, bf16[4,4,3,256]{3,1,2,0:T(4,128)(2,1)S(1)}, bf16[4,4,256,128]{3,2,1,0:T(8,128)(2,1)S(1)}, /*index=5*/s32[]{:T(128)}) while((s32[]{:T(128)}, f32[4,4,256,128]{3,2,1,0:T(8,128)}, f32[1,4,1,1]{1,3,2,0:T(1,128)S(1)}, ...), condition=%wide.region_1.2_spmd, body=%wide.region_0.1_spmd.sunk | while | flops 273159168 | bytes 3466345 | solution.py:68
  34.3 74.6 %all-reduce.1 = bf16[32,8192]{1,0:T(8,128)(2,1)S(1)} all-reduce(f32[32,8192]{1,0:T(8,128)S(1)} %fusion.78), channel_id=1, replica_groups=mesh['group'=4,'dev'=8] {'dev'}, use_global_device_ids=true, to_apply=%region_10.11 | all-reduce | flops 262144 | bytes 1572864 | tf_op jit(solution)/shard_map/psum | solution.py:168
  110.0 2.8 %copy.67 = f32[2,8,256,128]{3,1,2,0:T(8,128)S(1)} copy(f32[2,8,256,128]{3,2,1,0:T(8,128)} %bitcast.216) | data formatting | bytes 4194304
  112.9 22.6 %while.27 = (s32[]{:T(128)}, f32[16,32768]{1,0:T(8,128)S(1)}, bf16[2,8,256,128]{3,2,1,0:T(8,128)(2,1)}, s32[2,8]{1,0:T(2,128)S(1)}, f32[1,4,1,1]{1,3,2,0:T(1,128...) while((s32[]{:T(128)}, f32[16,32768]{1,0:T(8,128)S(1)}, ...), condition=%wide.region_9.10_spmd, body=%wide.region_7.9_spmd.sunk | while | flops 1089484800 | bytes 16478605 | solution.py:132
  115.2 2.3 %fusion.141 = bf16[2,8,256,128]{3,2,1,0:T(8,128)(2,1)} fusion(bf16[2,8,256,128]{3,2,1,0:T(8,128)(2,1)} %get-tuple-element.456, s32[]{:T(128)S(6)} %copy.82, f32[8,256,256]{1,2,0:T(8,128)S(1)} %multiply_add_fusion.5, f32[4]{0:T(128)S(1)} %bitcast.229, bf16[8,256,128]{2,1,0:T(8,128)(2,1)S(1)} %get-tuple-element.424, bf16[4,128]{1,0:T(4,128)(2,1)S(1)} %fusion.138, ...), kind=kOutput, calls=%fused_computation.41.clone.1 | convolution fusion | flops 542638080 | bytes 3146804 | tf_op jit(solution)/shard_map/while/body/eval_jaxpr/nhqp,nhqc->npc/dot_general | solution.py:28
  117.5 1.9 %fusion.139 = f32[1,8,256,128]{3,2,1,0:T(8,128)S(1)} fusion(f32[8,256,256]{1,2,0:T(8,128)S(1)} %multiply_add_fusion.5, f32[4]{0:T(128)S(1)} %bitcast.230, bf16[4,128]{1,0:T(4,128)(2,1)S(1)} %fusion.138, bf16[8,256,128]{2,1,0:T(8,128)(2,1)S(1)} %get-tuple-element.423), kind=kOutput, calls=%fused_computation.36.clone.1 | convolution fusion | flops 542113792 | bytes 3671056 | tf_op jit(solution)/shard_map/while/body/eval_jaxpr/nhpq,nhqc->npc/dot_general | solution.py:28
  121.0 3.2 %scatter_fusion = f32[16,32768]{1,0:T(8,128)S(1)} fusion(f32[16,32768]{1,0:T(8,128)S(1)} %get-tuple-element.455, s32[8]{0:T(128)S(1)} %fusion.137, f32[8,32768]{1,0:T(8,128)} %bitcast_multiply_fusion.2), kind=kCustom, calls=%fused_computation.4.clone.1 | custom fusion | flops 262144 | bytes 3145760 | tf_op jit(solution)/shard_map/while/body/eval_jaxpr/scatter-add | solution.py:116
  126.5 2.3 %fusion.141 = bf16[2,8,256,128]{3,2,1,0:T(8,128)(2,1)} fusion(bf16[2,8,256,128]{3,2,1,0:T(8,128)(2,1)} %get-tuple-element.456, s32[]{:T(128)S(6)} %copy.82, f32[8,256,256]{1,2,0:T(8,128)S(1)} %multiply_add_fusion.5, f32[4]{0:T(128)S(1)} %bitcast.229, bf16[8,256,128]{2,1,0:T(8,128)(2,1)S(1)} %get-tuple-element.424, bf16[4,128]{1,0:T(4,128)(2,1)S(1)} %fusion.138, ...), kind=kOutput, calls=%fused_computation.41.clone.1 | convolution fusion | flops 542638080 | bytes 3146804 | tf_op jit(solution)/shard_map/while/body/eval_jaxpr/nhqp,nhqc->npc/dot_general | solution.py:28
  128.8 1.9 %fusion.139 = f32[1,8,256,128]{3,2,1,0:T(8,128)S(1)} fusion(f32[8,256,256]{1,2,0:T(8,128)S(1)} %multiply_add_fusion.5, f32[4]{0:T(128)S(1)} %bitcast.230, bf16[4,128]{1,0:T(4,128)(2,1)S(1)} %fusion.138, bf16[8,256,128]{2,1,0:T(8,128)(2,1)S(1)} %get-tuple-element.423), kind=kOutput, calls=%fused_computation.36.clone.1 | convolution fusion | flops 542113792 | bytes 3671056 | tf_op jit(solution)/shard_map/while/body/eval_jaxpr/nhpq,nhqc->npc/dot_general | solution.py:28
  132.3 3.2 %scatter_fusion = f32[16,32768]{1,0:T(8,128)S(1)} fusion(f32[16,32768]{1,0:T(8,128)S(1)} %get-tuple-element.455, s32[8]{0:T(128)S(1)} %fusion.137, f32[8,32768]{1,0:T(8,128)} %bitcast_multiply_fusion.2), kind=kCustom, calls=%fused_computation.4.clone.1 | custom fusion | flops 262144 | bytes 3145760 | tf_op jit(solution)/shard_map/while/body/eval_jaxpr/scatter-add | solution.py:116
  135.5 4.4 %all-to-all-start.2 = ((bf16[8,2,256,128]{3,2,1,0:T(8,128)(2,1)}), bf16[8,2,256,128]{3,2,1,0:T(8,128)(2,1)}, u32[]{:S(2)}, u32[]{:S(2)}) async-start(bf16[8,2,256,128]{3,2,1,0:T(8,128)(2,1)} %bitcast.56), calls=%async_computation.2 | async-start | bytes 2097152 | tf_op jit(solution)/shard_map/all_to_all | solution.py:144
  140.0 2.4 %fusion.55 = bf16[2048,128]{1,0:T(8,128)(2,1)} fusion(bf16[2048,128]{1,0:T(8,128)(2,1)} %reshape.359, bf16[128,128]{1,0:T(8,128)(2,1)S(1)} %copy-done.6), kind=kOutput, calls=%fused_computation.93 | convolution fusion | flops 69468160 | bytes 1081344 | tf_op jit(solution)/shard_map/dot_general | solution.py:169
  142.4 2.1 %reshape.361 = bf16[32,8192]{1,0:T(8,128)(2,1)} reshape(bf16[2048,128]{1,0:T(8,128)(2,1)} %fusion.55) | data formatting | bytes 1048576 | tf_op jit(solution)/shard_map/reshape | solution.py:172
  145.6 7.2 %all_gather.3 = bf16[32,8192]{1,0:T(8,128)(2,1)S(1)} all-gather(bf16[8,8192]{1,0:T(8,128)(2,1)S(1)} %fusion.44), channel_id=1, replica_groups=mesh['group'=4,'dev'=8] {'group'}, dimensions={0}, use_global_device_ids=true | all-gather | bytes 655360 | tf_op jit(solution)/shard_map/all_gather | solution.py:176
  154.1 2.3 %fusion.106 = f32[2048,128]{1,0:T(8,128)} fusion(bf16[2048,128]{1,0:T(8,128)(2,1)} %fusion.55, bf16[128,128]{1,0:T(8,128)(2,1)} %param.28), kind=kOutput, calls=%fused_computation.189 | convolution fusion | flops 67108864 | bytes 1605632 | tf_op jit(solution)/shard_map/dot_general | solution.py:186
  156.4 2.4 %reshape.360 = f32[32,8192]{1,0:T(8,128)} reshape(f32[2048,128]{1,0:T(8,128)} %fusion.106) | data formatting | bytes 2097152 | tf_op jit(solution)/shard_map/reshape | solution.py:188
  158.8 1.9 %fusion.47 = bf16[2,8,64,128]{3,1,2,0:T(8,128)(2,1)S(1)} fusion(f32[32,8192]{1,0:T(8,128)} %reshape.360, bf16[8,8192]{1,0:T(8,128)(2,1)S(1)} %reshape.363, s32[32]{0:T(128)S(1)} %copy-done.5, s32[16]{0:T(128)S(1)} %copy-done.4), kind=kOutput, calls=%fused_computation.85 | convolution fusion | flops 15336192 | bytes 1441984 | tf_op jit(solution)/shard_map/dot_general | solution.py:195
  160.7 2.2 %fusion.46 = bf16[16,256,128]{1,2,0:T(8,128)(2,1)} fusion(bf16[16,64,128]{2,1,0:T(8,128)(2,1)S(1)} %bitcast.218, bf16[256,64]{0,1:T(8,128)(2,1)} %param.30), kind=kOutput, calls=%fused_computation.83 | convolution fusion | flops 67633152 | bytes 1343488 | tf_op jit(solution)/shard_map/bs,nsc->nbc/dot_general | solution.py:198
  162.9 2.3 %copy.41 = bf16[16,256,128]{2,1,0:T(8,128)(2,1)} copy(bf16[16,256,128]{1,2,0:T(8,128)(2,1)} %fusion.46) | data formatting | bytes 2097152 | tf_op jit(solution)/shard_map/convert_element_type | solution.py:204
  165.2 3.3 %fusion.43 = f32[16,32768]{1,0:T(8,128)} fusion(f32[16,32768]{1,0:T(8,128)S(1)} %get-tuple-element.203, bf16[2,8,256,128]{3,2,1,0:T(8,128)(2,1)} %bitcast.73, s32[16]{0:T(128)S(1)} %get-tuple-element.252, pred[16]{0:T(512)(128)(4,1)S(1)} %get-tuple-element.251), kind=kOutput, calls=%fused_computation.70 | convolution fusion | flops 17826304 | bytes 5242960 | tf_op jit(solution)/shard_map/dot_general | solution.py:151
  170.3 2.6 %fusion.45 = bf16[4096,128]{1,0:T(8,128)(2,1)} fusion(f32[4096,128]{1,0:T(8,128)S(1)} %mul.354, bf16[4096,128]{1,0:T(8,128)(2,1)} %bitcast.215, bf16[128,128]{1,0:T(8,128)(2,1)S(1)} %copy-done.2), kind=kOutput, calls=%fused_computation.77 | convolution fusion | flops 135266304 | bytes 4227072 | tf_op jit(solution)/shard_map/dot_general | solution.py:205
  (109 shorter events, 32.0 us)
Async XLA Ops:
  0.0 11.6 %copy-start = (bf16[4096,128]{1,0:T(8,128)(2,1)S(1)}, bf16[4096,128]{1,0:T(8,128)(2,1)}, u32[]{:S(2)}) copy-start(bf16[4096,128]{1,0:T(8,128)(2,1)} %param.18) | copy-start | bytes 3145732
  4.3 13.9 %all-to-all-start = ((bf16[8,2,3,256]{3,1,2,0:T(2,128)(2,1)}), bf16[8,2,3,256]{3,1,2,0:T(2,128)(2,1)S(1)}, u32[]{:S(2)}, u32[]{:S(2)}) async-start(bf16[8,2,3,256]{3,1,2,0:T(2,128)(2,1)} %copy_multiply_fusion), calls=%async_computation | async-start | bytes 49152 | tf_op jit(solution)/shard_map/all_to_all | solution.py:120
  12.8 1.9 %copy-start.8 = (f32[4]{0:T(128)S(1)}, f32[4]{0:T(128)}, u32[]{:S(2)}) copy-start(f32[4]{0:T(128)} %param.23) | copy-start | bytes 52
  12.8 1.9 %copy-start.1 = (bf16[3,4096]{1,0:T(4,128)(2,1)S(1)}, bf16[3,4096]{1,0:T(4,128)(2,1)}, u32[]{:S(2)}) copy-start(bf16[3,4096]{1,0:T(4,128)(2,1)} %param.19) | copy-start | bytes 73732
  18.3 94.6 %all-to-all-start.1 = ((bf16[8,2,256,128]{3,2,1,0:T(8,128)(2,1)}), bf16[8,2,256,128]{3,2,1,0:T(8,128)(2,1)}, u32[]{:S(2)}, u32[]{:S(2)}) async-start(bf16[8,2,256,128]{3,2,1,0:T(8,128)(2,1)} %broadcast_multiply_fusion), calls=%async_computation.1 | async-start | bytes 2097152 | tf_op jit(solution)/shard_map/all_to_all | solution.py:119
  31.3 2.5 %copy-start.3 = (bf16[64,256]{1,0:T(8,128)(2,1)S(1)}, bf16[64,256]{1,0:T(8,128)(2,1)}, u32[]{:S(2)}) copy-start(bf16[64,256]{1,0:T(8,128)(2,1)} %param.25) | copy-start | bytes 98308
  31.3 2.8 %copy-start.4 = (s32[16]{0:T(128)S(1)}, s32[16]{0:T(128)}, u32[]{:S(2)}) copy-start(s32[16]{0:T(128)} %param.21) | copy-start | bytes 196
  135.5 4.5 %copy-start.6 = (bf16[128,128]{1,0:T(8,128)(2,1)S(1)}, bf16[128,128]{1,0:T(8,128)(2,1)}, u32[]{:S(2)}) copy-start(bf16[128,128]{1,0:T(8,128)(2,1)} %param.26) | copy-start | bytes 98308
  135.5 29.7 %all-to-all-start.2 = ((bf16[8,2,256,128]{3,2,1,0:T(8,128)(2,1)}), bf16[8,2,256,128]{3,2,1,0:T(8,128)(2,1)}, u32[]{:S(2)}, u32[]{:S(2)}) async-start(bf16[8,2,256,128]{3,2,1,0:T(8,128)(2,1)} %bitcast.56), calls=%async_computation.2 | async-start | bytes 2097152 | tf_op jit(solution)/shard_map/all_to_all | solution.py:144
  140.0 4.4 %copy-start.5 = (s32[32]{0:T(128)S(1)}, s32[32]{0:T(128)}, u32[]{:S(2)}) copy-start(s32[32]{0:T(128)} %param.22) | copy-start | bytes 388
  142.4 11.4 %copy-start.7 = (bf16[128,128]{1,0:T(8,128)(2,1)S(1)}, bf16[128,128]{1,0:T(8,128)(2,1)}, u32[]{:S(2)}) copy-start(bf16[128,128]{1,0:T(8,128)(2,1)} %param.27) | copy-start | bytes 98308
  168.5 1.7 %copy-start.2 = (bf16[128,128]{1,0:T(8,128)(2,1)S(1)}, bf16[128,128]{1,0:T(8,128)(2,1)}, u32[]{:S(2)}) copy-start(bf16[128,128]{1,0:T(8,128)(2,1)} %param.31) | copy-start | bytes 98308
where the time goes:
time: 174 us; the launch traced here: 173 us
  blocking collectives  81.8 us (47%)
  matrix products  33.8 us (19%)
  local copies, waits for them, and re-layouts  19.9 us (11%)
  other arithmetic  17.3 us (10%)
  starting transfers between devices  16 us (9%)
  waiting for transfers between devices  3.51 us (2%)
    psum x1, blocking collectives, per_device(): lax.psum(partial_two, 'dev').astype(jnp.bfloat16).reshape(-1, channels)  74.6 us
    dot_general x8, matrix products, apply_table(): return jnp.einsum(form, kernel, masked, preferred_element_type=jnp.float32)  15 us
    all_to_all x1, starting transfers between devices, per_device(): lax.all_to_all(picked_coords, 'dev', split_axis=0, concat_axis=0, tiled=T...  7.31 us
    all_gather x1, blocking collectives, per_device(): three_all = lax.all_gather(level_three, 'group', axis=0, tiled=True)  7.17 us
    scatter-add x2, other arithmetic, accumulate(): return running.at[index].add(flat_side)  6.32 us
    all_to_all x1, starting transfers between devices, per_device(): lax.all_to_all(side_second.reshape(dev_count, CAP, blk_points, channels),...  4.44 us
    all_to_all x1, starting transfers between devices, per_device(): lax.all_to_all(picked_values, 'dev', split_axis=0, concat_axis=0, tiled=T...  4.25 us
    add x6, other arithmetic, kernel_table(): distance = delta_x * delta_x + delta_y * delta_y + delta_z * delta_z  3.65 us
  transfers between devices with their start and end apart: 3, of which 1 were waited for; matrix products, arithmetic and copies ran while one was open for 21% of the time, Pallas kernels for 0%

commit v1 on v0

--- a/solution.py
+++ b/solution.py
@@ -165,7 +165,11 @@
         jnp.bfloat16
     )
     partial_two = jnp.dot(select_all, level_one, preferred_element_type=jnp.float32)
-    flat = lax.psum(partial_two, "dev").astype(jnp.bfloat16).reshape(-1, channels)
+    flat = (
+        jnp.sum(lax.all_gather(partial_two, "dev"), axis=0)
+        .astype(jnp.bfloat16)
+        .reshape(-1, channels)
+    )
     result = jax.nn.gelu(jnp.dot(flat, w_two, preferred_element_type=jnp.float32)).astype(
         jnp.bfloat16
     )

time: 174 us -> 230 us (1.32)
  waiting for transfers between devices: 3.51 us -> 112 us
  blocking collectives: 81.8 us -> 7.15 us
  between operations: 0.28 us -> 13.6 us
  other arithmetic: 17.3 us -> 22.2 us
    psum x1 -> x0, blocking collectives: 74.6 us -> none  [per_device(): lax.psum(partial_two, 'dev').astype(jnp.bfloat16).reshape(-1, channels)]
    all_to_all x1, waiting for transfers between devices: 0.01 us -> 54.7 us  [per_device(): lax.all_to_all(side_second.reshape(dev_count, CAP, blk_points, channels),...]
    all_to_all x1, waiting for transfers between devices: 0.01 us -> 37.5 us  [per_device(): lax.all_to_all(picked_values, 'dev', split_axis=0, concat_axis=0, tiled=T...]
    all_gather x0 -> x1, waiting for transfers between devices: none -> 18.5 us  [per_device(): lax.all_gather(partial_two, 'dev')]
    reduce_sum x0 -> x1, other arithmetic: none -> 4.75 us  [per_device(): jnp.sum(lax.all_gather(partial_two, 'dev'), axis=0).astype(jnp.bfloat16)]
    all_to_all x1, waiting for transfers between devices: 3.51 us -> 1.13 us  [per_device(): lax.all_to_all(picked_coords, 'dev', split_axis=0, concat_axis=0, tiled=T...]
  transfers between devices with their start and end apart: 3 -> 4, of which waited for: 1 -> 4; matrix products, arithmetic and copies ran while one was open for 21% -> 21% of each run, Pallas kernels for 0% -> 0%
where the time goes in v1:
time: 230 us; the launch traced here: 228 us
  waiting for transfers between devices  112 us (49%)
  matrix products  35.5 us (15%)
  other arithmetic  22.2 us (10%)
  local copies, waits for them, and re-layouts  21.2 us (9%)
  starting transfers between devices  16.6 us (7%)
  between operations  13.6 us (6%)
  blocking collectives  7.15 us (3%)
    all_to_all x1, waiting for transfers between devices, per_device(): lax.all_to_all(side_second.reshape(dev_count, CAP, blk_points, channels),...  54.7 us
    all_to_all x1, waiting for transfers between devices, per_device(): lax.all_to_all(picked_values, 'dev', split_axis=0, concat_axis=0, tiled=T...  37.5 us
    all_gather x1, waiting for transfers between devices, per_device(): lax.all_gather(partial_two, 'dev')  18.5 us
    dot_general x8, matrix products, apply_table(): return jnp.einsum(form, kernel, masked, preferred_element_type=jnp.float32)  15.1 us
    all_to_all x1, starting transfers between devices, per_device(): lax.all_to_all(picked_coords, 'dev', split_axis=0, concat_axis=0, tiled=T...  7.31 us
    all_gather x1, blocking collectives, per_device(): three_all = lax.all_gather(level_three, 'group', axis=0, tiled=True)  7.15 us
    scatter-add x2, other arithmetic, accumulate(): return running.at[index].add(flat_side)  6.32 us
    all_to_all x1, starting transfers between devices, per_device(): lax.all_to_all(picked_values, 'dev', split_axis=0, concat_axis=0, tiled=T...  4.84 us
  transfers between devices with their start and end apart: 4, of which 4 were waited for; matrix products, arithmetic and copies ran while one was open for 21% of the time, Pallas kernels for 0%

profile of v1, /device:TPU:0, one launch (start us, length us, event | category | flops | bytes accessed | tf_op | source)
XLA Modules:
  0.0 228.4 jit_solution(8930580604972396798)
XLA Ops:
  10.9 7.3 %all-to-all-start = ((bf16[8,2,3,256]{3,1,2,0:T(2,128)(2,1)}), bf16[8,2,3,256]{3,1,2,0:T(2,128)(2,1)S(1)}, u32[]{:S(2)}, u32[]{:S(2)}) async-start(bf16[8,2,3,256]{3,1,2,0:T(2,128)(2,1)} %copy_multiply_fusion), calls=%async_computation | async-start | bytes 49152 | tf_op jit(solution)/shard_map/all_to_all | solution.py:120
  24.8 4.8 %all-to-all-start.1 = ((bf16[8,2,256,128]{3,2,1,0:T(8,128)(2,1)}), bf16[8,2,256,128]{3,2,1,0:T(8,128)(2,1)}, u32[]{:S(2)}, u32[]{:S(2)}) async-start(bf16[8,2,256,128]{3,2,1,0:T(8,128)(2,1)} %broadcast_multiply_fusion), calls=%async_computation.1 | async-start | bytes 2097152 | tf_op jit(solution)/shard_map/all_to_all | solution.py:119
  29.6 8.8 %while.26 = (s32[]{:T(128)}, f32[4,4,256,128]{3,2,1,0:T(8,128)}, f32[1,4,1,1]{1,3,2,0:T(1,128)S(1)}, bf16[4,4,3,256]{3,1,2,0:T(4,128)(2,1)S(1)}, bf16[4,4,256,128]{3,2,1,0:T(8,128)(2,1)S(1)}, /*index=5*/s32[]{:T(128)}) while((s32[]{:T(128)}, f32[4,4,256,128]{3,2,1,0:T(8,128)}, f32[1,4,1,1]{1,3,2,0:T(1,128)S(1)}, ...), condition=%wide.region_1.2_spmd, body=%wide.region_0.1_spmd.sunk | while | flops 273159168 | bytes 3466345 | solution.py:68
  40.9 2.8 %copy.67 = f32[2,8,256,128]{3,1,2,0:T(8,128)S(1)} copy(f32[2,8,256,128]{3,2,1,0:T(8,128)} %bitcast.218) | data formatting | bytes 4194304
  43.8 37.5 %all-to-all-done.1 = bf16[8,2,256,128]{3,2,1,0:T(8,128)(2,1)} async-done(((bf16[8,2,256,128]{3,2,1,0:T(8,128)(2,1)}), bf16[8,2,256,128]{3,2,1,0:T(8,128)(2,1)}, u32[]{:S(2)}, u32[]{:S(2)}) %all-to-all-start.1) | async-done | bytes 1048608 | tf_op jit(solution)/shard_map/all_to_all | solution.py:119
  81.3 23.0 %while.27 = (s32[]{:T(128)}, f32[16,32768]{1,0:T(8,128)S(1)}, bf16[2,8,256,128]{3,2,1,0:T(8,128)(2,1)}, s32[2,8]{1,0:T(2,128)S(1)}, f32[1,4,1,1]{1,3,2,0:T(1,128...) while((s32[]{:T(128)}, f32[16,32768]{1,0:T(8,128)S(1)}, ...), condition=%wide.region_9.10_spmd, body=%wide.region_7.9_spmd.sunk | while | flops 1089484800 | bytes 16478605 | solution.py:132
  83.5 2.3 %fusion.141 = bf16[2,8,256,128]{3,2,1,0:T(8,128)(2,1)} fusion(bf16[2,8,256,128]{3,2,1,0:T(8,128)(2,1)} %get-tuple-element.456, s32[]{:T(128)S(6)} %copy.82, f32[8,256,256]{1,2,0:T(8,128)S(1)} %multiply_add_fusion.5, f32[4]{0:T(128)S(1)} %bitcast.231, bf16[8,256,128]{2,1,0:T(8,128)(2,1)S(1)} %get-tuple-element.424, bf16[4,128]{1,0:T(4,128)(2,1)S(1)} %fusion.138, ...), kind=kOutput, calls=%fused_computation.41.clone.1 | convolution fusion | flops 542638080 | bytes 3146804 | tf_op jit(solution)/shard_map/while/body/eval_jaxpr/nhqp,nhqc->npc/dot_general | solution.py:28
  89.4 3.2 %scatter_fusion = f32[16,32768]{1,0:T(8,128)S(1)} fusion(f32[16,32768]{1,0:T(8,128)S(1)} %get-tuple-element.455, s32[8]{0:T(128)S(1)} %fusion.137, f32[8,32768]{1,0:T(8,128)} %bitcast_multiply_fusion.2), kind=kCustom, calls=%fused_computation.4.clone.1 | custom fusion | flops 262144 | bytes 3145760 | tf_op jit(solution)/shard_map/while/body/eval_jaxpr/scatter-add | solution.py:116
  95.2 2.3 %fusion.141 = bf16[2,8,256,128]{3,2,1,0:T(8,128)(2,1)} fusion(bf16[2,8,256,128]{3,2,1,0:T(8,128)(2,1)} %get-tuple-element.456, s32[]{:T(128)S(6)} %copy.82, f32[8,256,256]{1,2,0:T(8,128)S(1)} %multiply_add_fusion.5, f32[4]{0:T(128)S(1)} %bitcast.231, bf16[8,256,128]{2,1,0:T(8,128)(2,1)S(1)} %get-tuple-element.424, bf16[4,128]{1,0:T(4,128)(2,1)S(1)} %fusion.138, ...), kind=kOutput, calls=%fused_computation.41.clone.1 | convolution fusion | flops 542638080 | bytes 3146804 | tf_op jit(solution)/shard_map/while/body/eval_jaxpr/nhqp,nhqc->npc/dot_general | solution.py:28
  101.1 3.2 %scatter_fusion = f32[16,32768]{1,0:T(8,128)S(1)} fusion(f32[16,32768]{1,0:T(8,128)S(1)} %get-tuple-element.455, s32[8]{0:T(128)S(1)} %fusion.137, f32[8,32768]{1,0:T(8,128)} %bitcast_multiply_fusion.2), kind=kCustom, calls=%fused_computation.4.clone.1 | custom fusion | flops 262144 | bytes 3145760 | tf_op jit(solution)/shard_map/while/body/eval_jaxpr/scatter-add | solution.py:116
  104.3 4.4 %all-to-all-start.2 = ((bf16[8,2,256,128]{3,2,1,0:T(8,128)(2,1)}), bf16[8,2,256,128]{3,2,1,0:T(8,128)(2,1)}, u32[]{:S(2)}, u32[]{:S(2)}) async-start(bf16[8,2,256,128]{3,2,1,0:T(8,128)(2,1)} %bitcast.56), calls=%async_computation.2 | async-start | bytes 2097152 | tf_op jit(solution)/shard_map/all_to_all | solution.py:144
  108.7 54.7 %all-to-all-done.2 = bf16[8,2,256,128]{3,2,1,0:T(8,128)(2,1)} async-done(((bf16[8,2,256,128]{3,2,1,0:T(8,128)(2,1)}), bf16[8,2,256,128]{3,2,1,0:T(8,128)(2,1)}, u32[]{:S(2)}, u32[]{:S(2)}) %all-to-all-start.2) | async-done | bytes 1048608 | tf_op jit(solution)/shard_map/all_to_all | solution.py:144
  163.4 3.3 %fusion.43 = f32[16,32768]{1,0:T(8,128)} fusion(f32[16,32768]{1,0:T(8,128)S(1)} %get-tuple-element.203, bf16[2,8,256,128]{3,2,1,0:T(8,128)(2,1)} %bitcast.74, s32[16]{0:T(128)S(1)} %get-tuple-element.252, pred[16]{0:T(512)(128)(4,1)S(1)} %get-tuple-element.251), kind=kOutput, calls=%fused_computation.70 | convolution fusion | flops 17826304 | bytes 5242960 | tf_op jit(solution)/shard_map/dot_general | solution.py:151
  168.5 18.5 %all-gather.3.cloned.1.call-done = f32[256,8192]{1,0:T(8,128)} async-done(((f32[32,8192]{1,0:T(8,128)}), f32[256,8192]{1,0:T(8,128)}) %all-gather.3.cloned.1.call-update) | async-done | bytes 8388624 | tf_op jit(solution)/shard_map/all_gather | solution.py:169
  186.9 4.8 %reduce_sum.45 = bf16[32,8192]{1,0:T(8,128)(2,1)} reduce(f32[8,32,8192]{2,1,0:T(8,128)} %bitcast.215, f32[]{:T(128)} %constant.192.clone.1), dimensions={0}, to_apply=%region_10.11 | reduce | flops 1835008 | bytes 8912900 | tf_op jit(solution)/shard_map/reduce_sum | solution.py:169
  191.7 2.1 convert_element_type.146
  193.7 2.3 %fusion.55 = bf16[2048,128]{1,0:T(8,128)(2,1)} fusion(bf16[2048,128]{1,0:T(8,128)(2,1)} %convert_element_type.146, bf16[128,128]{1,0:T(8,128)(2,1)S(1)} %copy-done.6), kind=kOutput, calls=%fused_computation.93 | convolution fusion | flops 69468160 | bytes 1081344 | tf_op jit(solution)/shard_map/dot_general | solution.py:173
  196.1 2.1 reshape.360
  199.4 7.2 %all_gather.11 = bf16[32,8192]{1,0:T(8,128)(2,1)S(1)} all-gather(bf16[8,8192]{1,0:T(8,128)(2,1)S(1)} %fusion.44), channel_id=1, replica_groups=mesh['group'=4,'dev'=8] {'group'}, dimensions={0}, use_global_device_ids=true | all-gather | bytes 655360 | tf_op jit(solution)/shard_map/all_gather | solution.py:180
  207.8 2.3 %fusion.106 = f32[2048,128]{1,0:T(8,128)} fusion(bf16[2048,128]{1,0:T(8,128)(2,1)} %fusion.55, bf16[128,128]{1,0:T(8,128)(2,1)} %param.28), kind=kOutput, calls=%fused_computation.189 | convolution fusion | flops 67108864 | bytes 1605632 | tf_op jit(solution)/shard_map/dot_general | solution.py:190
  210.1 2.4 %reshape.359 = f32[32,8192]{1,0:T(8,128)} reshape(f32[2048,128]{1,0:T(8,128)} %fusion.106) | data formatting | bytes 2097152 | tf_op jit(solution)/shard_map/reshape | solution.py:192
  214.5 2.2 fusion.46
  216.7 2.3 copy.41
  218.9 2.6 %fusion.45 = bf16[4096,128]{1,0:T(8,128)(2,1)} fusion(f32[4096,128]{1,0:T(8,128)S(1)} %mul.354, bf16[4096,128]{1,0:T(8,128)(2,1)} %bitcast.217, bf16[128,128]{1,0:T(8,128)(2,1)S(1)} %copy-done.3), kind=kOutput, calls=%fused_computation.77 | convolution fusion | flops 135266304 | bytes 4227072 | tf_op jit(solution)/shard_map/dot_general | solution.py:209
  (112 shorter events, 40.0 us)
Async XLA Ops:
  6.5 11.7 %copy-start = (bf16[4096,128]{1,0:T(8,128)(2,1)S(1)}, bf16[4096,128]{1,0:T(8,128)(2,1)}, u32[]{:S(2)}) copy-start(bf16[4096,128]{1,0:T(8,128)(2,1)} %param.18) | copy-start | bytes 3145732
  6.5 14.7 %copy-start.2 = (bf16[128,128]{1,0:T(8,128)(2,1)S(1)}, bf16[128,128]{1,0:T(8,128)(2,1)}, u32[]{:S(2)}) copy-start(bf16[128,128]{1,0:T(8,128)(2,1)} %param.24) | copy-start | bytes 98308
  10.9 13.9 %all-to-all-start = ((bf16[8,2,3,256]{3,1,2,0:T(2,128)(2,1)}), bf16[8,2,3,256]{3,1,2,0:T(2,128)(2,1)S(1)}, u32[]{:S(2)}, u32[]{:S(2)}) async-start(bf16[8,2,3,256]{3,1,2,0:T(2,128)(2,1)} %copy_multiply_fusion), calls=%async_computation | async-start | bytes 49152 | tf_op jit(solution)/shard_map/all_to_all | solution.py:120
  18.2 168.7 %all-gather.3.cloned.1.call-start = ((), (), s32[]{:S(2)}) async-start(), calls=%async_computation.3 | async-start | bytes 9437184 | tf_op jit(solution)/shard_map/all_gather | solution.py:169
  21.7 2.0 copy-start.8
  21.7 2.0 copy-start.1
  24.8 56.5 %all-to-all-start.1 = ((bf16[8,2,256,128]{3,2,1,0:T(8,128)(2,1)}), bf16[8,2,256,128]{3,2,1,0:T(8,128)(2,1)}, u32[]{:S(2)}, u32[]{:S(2)}) async-start(bf16[8,2,256,128]{3,2,1,0:T(8,128)(2,1)} %broadcast_multiply_fusion), calls=%async_computation.1 | async-start | bytes 2097152 | tf_op jit(solution)/shard_map/all_to_all | solution.py:119
  104.3 59.1 %all-to-all-start.2 = ((bf16[8,2,256,128]{3,2,1,0:T(8,128)(2,1)}), bf16[8,2,256,128]{3,2,1,0:T(8,128)(2,1)}, u32[]{:S(2)}, u32[]{:S(2)}) async-start(bf16[8,2,256,128]{3,2,1,0:T(8,128)(2,1)} %bitcast.56), calls=%async_computation.2 | async-start | bytes 2097152 | tf_op jit(solution)/shard_map/all_to_all | solution.py:144
  186.9 6.8 %copy-start.6 = (bf16[128,128]{1,0:T(8,128)(2,1)S(1)}, bf16[128,128]{1,0:T(8,128)(2,1)}, u32[]{:S(2)}) copy-start(bf16[128,128]{1,0:T(8,128)(2,1)} %param.26) | copy-start | bytes 98308
  193.7 4.4 %copy-start.5 = (s32[32]{0:T(128)S(1)}, s32[32]{0:T(128)}, u32[]{:S(2)}) copy-start(s32[32]{0:T(128)} %param.22) | copy-start | bytes 388
  196.1 11.4 %copy-start.7 = (bf16[128,128]{1,0:T(8,128)(2,1)S(1)}, bf16[128,128]{1,0:T(8,128)(2,1)}, u32[]{:S(2)}) copy-start(bf16[128,128]{1,0:T(8,128)(2,1)} %param.27) | copy-start | bytes 98308
  207.7 4.8 %copy-start.4 = (s32[16]{0:T(128)S(1)}, s32[16]{0:T(128)}, u32[]{:S(2)}) copy-start(s32[16]{0:T(128)} %param.21) | copy-start | bytes 196
  214.4 4.5 %copy-start.3 = (bf16[128,128]{1,0:T(8,128)(2,1)S(1)}, bf16[128,128]{1,0:T(8,128)(2,1)}, u32[]{:S(2)}) copy-start(bf16[128,128]{1,0:T(8,128)(2,1)} %param.31) | copy-start | bytes 98308
Sparse Core Ops, SparseCore 0:
  21.4 165.4 all-gather.2
